TPU v7x, 128 devices: a whole 4x4x4 slice. The times are simulated.
128 devices in a mesh: row: 16 (over y, z), col: 8 (over x, core).
Axes of the slice: x: 4, y: 4, z: 4, core: 2. Of those that a mesh axis runs over, the one named last changes fastest.
Arguments:
- blocks: bfloat16 [16, 8, 128, 4096], P('row', 'col'), may hold values from -0.25 to 0.25
- block_row: int32 [16, 8, 128], P('row', 'col'), may hold values from 0 to 15
- block_col: int32 [16, 8, 128], P('row', 'col'), may hold values from 0 to 31
- counts: int32 [16, 8], P('row', 'col'), may hold values from 0 to 128, as said below
- vectors: float32 [256, 4096], P(('col', 'row')), may hold values from -6 to 6
- row_mass: float32 [256, 64], P(('row', 'col')), may hold values from 0.25 to 4
- col_mass: float32 [256, 64], P(('col', 'row')), may hold values from 0.25 to 4
Outputs:
- subspace: float32 [256, 4096], P(('col', 'row'))
Inputs may be any that keep to these rules, and one draw needn't show every extreme that they name: `counts`: in every row panel one tile uses all 128 slots; every other tile uses at most 8.
All inputs are finite; a program needn't handle non-finite values.
Results may differ from a plain program's by a relative error of at most 0.0085.
Values may be sent and summed in bfloat16 or wider, within the bound.
A program may use at most 64 MiB of HBM per device.

v0:
```python
import jax
import jax.numpy as jnp
from jax import lax
from jax.sharding import PartitionSpec as P

ITERS = 4


def rotate(projected, gram):
    lower = jnp.linalg.cholesky(gram)
    inverse = lax.linalg.triangular_solve(
        lower, jnp.eye(gram.shape[0], dtype=jnp.float32), left_side=True, lower=True
    )
    return jnp.einsum(
        "kl,bli->bki",
        inverse,
        projected,
        precision=lax.Precision.HIGHEST,
        preferred_element_type=jnp.float32,
    )


def local_gram(projected):
    return jnp.einsum(
        "bki,bli->kl",
        projected,
        projected,
        precision=lax.Precision.HIGHEST,
        preferred_element_type=jnp.float32,
    )


def per_device(blocks, block_row, block_col, counts, vectors, row_mass, col_mass):
    tile = blocks[0, 0]
    n_cap = tile.shape[0]
    bsize = row_mass.shape[1]
    vecs = vectors.shape[1] // bsize
    own = vectors.shape[0]
    n_row = lax.axis_size("row")
    n_col = lax.axis_size("col")
    row_panel = own * n_col
    col_panel = own * n_row
    total_boxes = float(own * bsize * n_row * n_col)
    rows_idx = block_row[0, 0]
    cols_idx = block_col[0, 0]
    live = jnp.arange(n_cap) < counts[0, 0]
    fwd_ids = jnp.where(live, rows_idx, row_panel)
    bwd_ids = jnp.where(live, cols_idx, col_panel)
    square = tile.reshape(n_cap, bsize, bsize)
    col_mass_panel = lax.all_gather(col_mass, "row", axis=0, tiled=True)
    row_mass_panel = lax.all_gather(row_mass, "col", axis=0, tiled=True)
    inv_col = 1.0 / jnp.sqrt(col_mass_panel)
    current = lax.all_gather(vectors, "row", axis=0, tiled=True).reshape(col_panel, vecs, bsize)
    for step in range(ITERS):
        scaled = (current * inv_col[:, None, :]).astype(jnp.bfloat16)
        forward_taken = jnp.take(scaled, cols_idx, axis=0)
        forward_product = jnp.einsum(
            "bij,bkj->bki", square, forward_taken, preferred_element_type=jnp.float32
        )
        forward_summed = jax.ops.segment_sum(forward_product, fwd_ids, num_segments=row_panel + 1)
        rows_sum = lax.psum(forward_summed[:row_panel], "col")
        weighted = (rows_sum * row_mass_panel[:, None, :]).astype(jnp.bfloat16)
        taken = jnp.take(weighted, rows_idx, axis=0)
        product = jnp.einsum("bij,bki->bkj", square, taken, preferred_element_type=jnp.float32)
        summed = jax.ops.segment_sum(product, bwd_ids, num_segments=col_panel + 1)
        cols_sum = lax.psum(summed[:col_panel], "row")
        projected = cols_sum * inv_col[:, None, :]
        gram = lax.psum(local_gram(projected), "col") / total_boxes
        current = rotate(projected, gram)
    me = lax.axis_index("row")
    mine = lax.dynamic_slice_in_dim(current, me * own, own, 0)
    return mine.reshape(own, vecs * bsize)


def solution(mesh):
    in_specs = (
        P("row", "col", None, None),
        P("row", "col", None),
        P("row", "col", None),
        P("row", "col"),
        P(("col", "row"), None),
        P(("row", "col"), None),
        P(("col", "row"), None),
    )
    out_specs = P(("col", "row"), None)
    return jax.shard_map(
        per_device, mesh=mesh, in_specs=in_specs, out_specs=out_specs, check_vma=False
    )
```

profile of v0, /device:TPU:0, one launch (start us, length us, event | category | flops | bytes accessed | tf_op | source)
XLA Modules:
  0.0 997.5 jit_solution(7439342869983005372)
XLA Ops:
  7.9 24.9 %all-gather.1 = f32[16,2,64]{2,1,0:T(2,128)S(1)} all-gather(f32[1,2,64]{2,1,0:T(2,128)} %bitcast.111), channel_id=1, replica_groups=mesh['row'=16,'col'=8] {'row'}, dimensions={0}, use_global_device_ids=true | all-gather | bytes 8704 | tf_op jit(solution)/shard_map/all_gather | solution.py:50
  32.8 23.5 %all-gather = f32[16,2,4096]{2,1,0:T(2,128)S(1)} all-gather(f32[1,2,4096]{2,1,0:T(2,128)} %bitcast.110), channel_id=1, replica_groups=mesh['row'=16,'col'=8] {'row'}, dimensions={0}, use_global_device_ids=true | all-gather | bytes 557056 | tf_op jit(solution)/shard_map/all_gather | solution.py:53
  56.3 1.6 reshape.57
  58.6 3.0 copy.41
  62.3 1.4 multiply_convert_fusion
  63.6 2.1 gather_fusion
  65.8 4.8 fusion.14
  70.6 13.5 %scatter_fusion = f32[17,64,64]{2,1,0:T(8,128)S(1)} fusion(f32[17,64,64]{2,1,0:T(8,128)S(1)} %broadcast.82.clone.2, s32[128]{0:T(128)S(1)} %get-tuple-element.8, f32[128,64,64]{2,1,0:T(8,128)} %fusion.14), kind=kCustom, calls=%fused_computation.8 | custom fusion | flops 524288 | bytes 6291968 | tf_op jit(solution)/shard_map/scatter-add | solution.py:60
  85.1 10.7 %all-gather.2 = f32[8,2,64]{2,1,0:T(2,128)S(1)} all-gather(f32[1,2,64]{2,1,0:T(2,128)S(1)} %bitcast.112), channel_id=1, replica_groups=mesh['row'=16,'col'=8] {'col'}, dimensions={0}, use_global_device_ids=true | all-gather | bytes 4608 | tf_op jit(solution)/shard_map/all_gather | solution.py:51
  95.8 48.5 %all-reduce.9.cloned.1.call-done = f32[16,64,64]{2,1,0:T(8,128)} async-done(((f32[16,64,64]{2,1,0:T(8,128)}), f32[16,64,64]{2,1,0:T(8,128)}) %all-reduce.9.cloned.1.call-update) | async-done | bytes 262160 | tf_op jit(solution)/shard_map/psum | solution.py:61
  145.4 2.1 gather_fusion.1
  147.6 4.3 fusion.12
  152.0 13.5 %scatter_fusion.1 = f32[33,64,64]{2,1,0:T(8,128)S(1)} fusion(f32[33,64,64]{2,1,0:T(8,128)S(1)} %broadcast.81.clone.2, s32[128]{0:T(128)S(1)} %get-tuple-element.6, f32[128,64,64]{2,1,0:T(8,128)} %fusion.12), kind=kCustom, calls=%fused_computation.9 | custom fusion | flops 524288 | bytes 6291968 | tf_op jit(solution)/shard_map/scatter-add | solution.py:65
  165.5 1.1 slice.55
  166.7 86.6 %all-reduce.11.cloned.1.call-done = f32[32,64,64]{2,1,0:T(8,128)} async-done(((f32[32,64,64]{2,1,0:T(8,128)}), f32[32,64,64]{2,1,0:T(8,128)}) %all-reduce.11.cloned.1.call-update) | async-done | bytes 524304 | tf_op jit(solution)/shard_map/psum | solution.py:66
  253.2 2.7 convolution_bitcast_fusion.7
  256.0 24.8 %psum.86 = f32[64,64]{0,1:T(8,128)S(1)} all-reduce(f32[64,64]{0,1:T(8,128)S(1)} %convolution_bitcast_fusion.7), channel_id=1, replica_groups=mesh['row'=16,'col'=8] {'col'}, use_global_device_ids=true, to_apply=%region_4.7 | all-reduce | flops 4096 | bytes 32768 | tf_op jit(solution)/shard_map/psum | solution.py:68
  280.9 5.8 cholesky.74
  288.1 4.9 custom-call.8
  293.2 2.8 fusion.29
  296.0 1.3 copy.46
  297.3 2.1 gather_fusion.2
  299.5 4.8 fusion.10
  304.3 13.5 %scatter_fusion.2 = f32[17,64,64]{2,1,0:T(8,128)S(1)} fusion(f32[17,64,64]{2,1,0:T(8,128)S(1)} %broadcast.82.clone.1, s32[128]{0:T(128)S(1)} %get-tuple-element.8, f32[128,64,64]{2,1,0:T(8,128)} %fusion.10), kind=kCustom, calls=%fused_computation.10 | custom fusion | flops 524288 | bytes 6291968 | tf_op jit(solution)/shard_map/scatter-add | solution.py:60
  318.7 57.4 %all-reduce.13.cloned.1.call-done = f32[16,64,64]{2,1,0:T(8,128)} async-done(((f32[16,64,64]{2,1,0:T(8,128)}), f32[16,64,64]{2,1,0:T(8,128)}) %all-reduce.13.cloned.1.call-update) | async-done | bytes 262160 | tf_op jit(solution)/shard_map/psum | solution.py:61
  377.2 2.1 gather_fusion.3
  379.3 4.3 fusion.8
  383.7 13.5 %scatter_fusion.3 = f32[33,64,64]{2,1,0:T(8,128)S(1)} fusion(f32[33,64,64]{2,1,0:T(8,128)S(1)} %broadcast.81.clone.1, s32[128]{0:T(128)S(1)} %get-tuple-element.6, f32[128,64,64]{2,1,0:T(8,128)} %fusion.8), kind=kCustom, calls=%fused_computation.11 | custom fusion | flops 524288 | bytes 6291968 | tf_op jit(solution)/shard_map/scatter-add | solution.py:65
  397.3 1.1 slice.57
  398.4 86.6 %all-reduce.15.cloned.1.call-done = f32[32,64,64]{2,1,0:T(8,128)} async-done(((f32[32,64,64]{2,1,0:T(8,128)}), f32[32,64,64]{2,1,0:T(8,128)}) %all-reduce.15.cloned.1.call-update) | async-done | bytes 524304 | tf_op jit(solution)/shard_map/psum | solution.py:66
  485.1 2.7 convolution_bitcast_fusion.5
  487.8 24.4 %psum.89 = f32[64,64]{0,1:T(8,128)S(1)} all-reduce(f32[64,64]{0,1:T(8,128)S(1)} %convolution_bitcast_fusion.5), channel_id=1, replica_groups=mesh['row'=16,'col'=8] {'col'}, use_global_device_ids=true, to_apply=%region_11.16 | all-reduce | flops 4096 | bytes 32768 | tf_op jit(solution)/shard_map/psum | solution.py:68
  512.3 5.8 cholesky.85
  519.5 4.9 custom-call.9
  524.7 2.8 fusion.28
  527.5 1.3 copy.52
  528.8 2.1 gather_fusion.4
  530.9 4.8 fusion.6
  535.8 13.5 %scatter_fusion.4 = f32[17,64,64]{2,1,0:T(8,128)S(1)} fusion(f32[17,64,64]{2,1,0:T(8,128)S(1)} %broadcast.82.clone, s32[128]{0:T(128)S(1)} %get-tuple-element.8, f32[128,64,64]{2,1,0:T(8,128)} %fusion.6), kind=kCustom, calls=%fused_computation.12 | custom fusion | flops 524288 | bytes 6291968 | tf_op jit(solution)/shard_map/scatter-add | solution.py:60
  550.2 57.4 %all-reduce.17.cloned.1.call-done = f32[16,64,64]{2,1,0:T(8,128)} async-done(((f32[16,64,64]{2,1,0:T(8,128)}), f32[16,64,64]{2,1,0:T(8,128)}) %all-reduce.17.cloned.1.call-update) | async-done | bytes 262160 | tf_op jit(solution)/shard_map/psum | solution.py:61
  608.7 2.1 gather_fusion.5
  610.8 4.3 fusion.4
  615.2 13.5 %scatter_fusion.5 = f32[33,64,64]{2,1,0:T(8,128)S(1)} fusion(f32[33,64,64]{2,1,0:T(8,128)S(1)} %broadcast.81.clone, s32[128]{0:T(128)S(1)} %get-tuple-element.6, f32[128,64,64]{2,1,0:T(8,128)} %fusion.4), kind=kCustom, calls=%fused_computation.13 | custom fusion | flops 524288 | bytes 6291968 | tf_op jit(solution)/shard_map/scatter-add | solution.py:65
  629.9 86.6 %all-reduce.19.cloned.1.call-done = f32[32,64,64]{2,1,0:T(8,128)} async-done(((f32[32,64,64]{2,1,0:T(8,128)}), f32[32,64,64]{2,1,0:T(8,128)}) %all-reduce.19.cloned.1.call-update) | async-done | bytes 524304 | tf_op jit(solution)/shard_map/psum | solution.py:66
  716.6 2.7 convolution_bitcast_fusion.3
  719.3 24.5 %psum.92 = f32[64,64]{0,1:T(8,128)S(1)} all-reduce(f32[64,64]{0,1:T(8,128)S(1)} %convolution_bitcast_fusion.3), channel_id=1, replica_groups=mesh['row'=16,'col'=8] {'col'}, use_global_device_ids=true, to_apply=%region_16.21 | all-reduce | flops 4096 | bytes 32768 | tf_op jit(solution)/shard_map/psum | solution.py:68
  743.9 5.8 cholesky.96
  751.1 4.9 custom-call.10
  756.2 2.8 fusion.27
  759.0 1.3 copy.58
  760.3 2.1 gather_fusion.6
  762.5 4.8 fusion.2
  767.3 13.5 %scatter_fusion.6 = f32[17,64,64]{2,1,0:T(8,128)S(1)} fusion(f32[17,64,64]{2,1,0:T(8,128)S(1)} %broadcast.82, s32[128]{0:T(128)S(1)} %get-tuple-element.8, f32[128,64,64]{2,1,0:T(8,128)} %fusion.2), kind=kCustom, calls=%fused_computation.14 | custom fusion | flops 524288 | bytes 6291968 | tf_op jit(solution)/shard_map/scatter-add | solution.py:60
  781.7 57.4 %all-reduce.21.cloned.1.call-done = f32[16,64,64]{2,1,0:T(8,128)} async-done(((f32[16,64,64]{2,1,0:T(8,128)}), f32[16,64,64]{2,1,0:T(8,128)}) %all-reduce.21.cloned.1.call-update) | async-done | bytes 262160 | tf_op jit(solution)/shard_map/psum | solution.py:61
  840.2 2.1 gather_fusion.7
  842.3 4.3 fusion
  846.7 13.5 %scatter_fusion.7 = f32[33,64,64]{2,1,0:T(8,128)S(1)} fusion(f32[33,64,64]{2,1,0:T(8,128)S(1)} %broadcast.81, s32[128]{0:T(128)S(1)} %get-tuple-element.6, f32[128,64,64]{2,1,0:T(8,128)} %fusion), kind=kCustom, calls=%fused_computation.15 | custom fusion | flops 524288 | bytes 6291968 | tf_op jit(solution)/shard_map/scatter-add | solution.py:65
  860.3 1.1 slice.61
  861.4 86.7 %all-reduce.23.cloned.1.call-done = f32[32,64,64]{2,1,0:T(8,128)} async-done(((f32[32,64,64]{2,1,0:T(8,128)}), f32[32,64,64]{2,1,0:T(8,128)}) %all-reduce.23.cloned.1.call-update) | async-done | bytes 524304 | tf_op jit(solution)/shard_map/psum | solution.py:66
  948.1 2.7 convolution_bitcast_fusion.1
  950.8 24.5 %psum.95 = f32[64,64]{0,1:T(8,128)S(1)} all-reduce(f32[64,64]{0,1:T(8,128)S(1)} %convolution_bitcast_fusion.1), channel_id=1, replica_groups=mesh['row'=16,'col'=8] {'col'}, use_global_device_ids=true, to_apply=%region_21.26 | all-reduce | flops 4096 | bytes 32768 | tf_op jit(solution)/shard_map/psum | solution.py:68
  975.4 5.8 cholesky.107
  982.6 4.9 custom-call.11
  987.8 1.8 fusion.38
  (89 shorter events, 19.6 us)
Async XLA Ops:
  6.5 51.4 %copy-start.4 = (bf16[1,1,128,4096]{3,2,1,0:T(8,128)(2,1)S(1)}, bf16[1,1,128,4096]{3,2,1,0:T(8,128)(2,1)}, u32[]{:S(2)}) copy-start(bf16[1,1,128,4096]{3,2,1,0:T(8,128)(2,1)} %param.14) | copy-start | bytes 3145732
  6.5 137.8 %all-reduce.9.cloned.1.call-start = ((), (), s32[]{:S(2)}) async-start(), calls=%async_computation | async-start | bytes 1048576 | tf_op jit(solution)/shard_map/psum | solution.py:61
  63.6 2.2 copy-start.6
  63.6 2.2 copy-start.7
  70.6 14.5 %copy-start.5 = (f32[2,64]{1,0:T(2,128)S(1)}, f32[2,64]{1,0:T(2,128)}, u32[]{:S(2)}) copy-start(f32[2,64]{1,0:T(2,128)} %param.19) | copy-start | bytes 1540
  85.0 168.2 %all-reduce.11.cloned.1.call-start = ((), (), s32[]{:S(2)}) async-start(), calls=%async_computation.1 | async-start | bytes 2097152 | tf_op jit(solution)/shard_map/psum | solution.py:66
  166.6 209.5 %all-reduce.13.cloned.1.call-start = ((), (), s32[]{:S(2)}) async-start(), calls=%async_computation.2 | async-start | bytes 1048576 | tf_op jit(solution)/shard_map/psum | solution.py:61
  253.2 40.0 %copy-start.1 = (f32[32,64,64]{2,1,0:T(8,128)S(1)}, f32[32,64,64]{2,1,0:T(8,128)}, u32[]{:S(2)}) copy-start(f32[32,64,64]{2,1,0:T(8,128)} %all-reduce.11.cloned.1.call-done) | copy-start | bytes 1572868
  318.7 166.4 %all-reduce.15.cloned.1.call-start = ((), (), s32[]{:S(2)}) async-start(), calls=%async_computation.3 | async-start | bytes 2097152 | tf_op jit(solution)/shard_map/psum | solution.py:66
  398.4 209.2 %all-reduce.17.cloned.1.call-start = ((), (), s32[]{:S(2)}) async-start(), calls=%async_computation.4 | async-start | bytes 1048576 | tf_op jit(solution)/shard_map/psum | solution.py:61
  485.1 39.6 %copy-start.2 = (f32[32,64,64]{2,1,0:T(8,128)S(1)}, f32[32,64,64]{2,1,0:T(8,128)}, u32[]{:S(2)}) copy-start(f32[32,64,64]{2,1,0:T(8,128)} %all-reduce.15.cloned.1.call-done) | copy-start | bytes 1572868
  550.1 166.4 %all-reduce.19.cloned.1.call-start = ((), (), s32[]{:S(2)}) async-start(), calls=%async_computation.5 | async-start | bytes 2097152 | tf_op jit(solution)/shard_map/psum | solution.py:66
  629.9 209.2 %all-reduce.21.cloned.1.call-start = ((), (), s32[]{:S(2)}) async-start(), calls=%async_computation.6 | async-start | bytes 1048576 | tf_op jit(solution)/shard_map/psum | solution.py:61
  716.6 39.7 %copy-start.3 = (f32[32,64,64]{2,1,0:T(8,128)S(1)}, f32[32,64,64]{2,1,0:T(8,128)}, u32[]{:S(2)}) copy-start(f32[32,64,64]{2,1,0:T(8,128)} %all-reduce.19.cloned.1.call-done) | copy-start | bytes 1572868
  781.7 166.4 %all-reduce.23.cloned.1.call-start = ((), (), s32[]{:S(2)}) async-start(), calls=%async_computation.7 | async-start | bytes 2097152 | tf_op jit(solution)/shard_map/psum | solution.py:66
  948.1 39.7 %copy-start = (f32[32,64,64]{2,1,0:T(8,128)S(1)}, f32[32,64,64]{2,1,0:T(8,128)}, u32[]{:S(2)}) copy-start(f32[32,64,64]{2,1,0:T(8,128)} %all-reduce.23.cloned.1.call-done) | copy-start | bytes 1572868
Sparse Core Ops, SparseCore 0:
  85.2 59.1 all-reduce.8
  166.7 86.4 all-reduce.10
  318.8 57.2 all-reduce.12
  398.5 86.4 all-reduce.14
  550.3 57.2 all-reduce.16
  630.0 86.5 all-reduce.18
  781.8 57.2 all-reduce.20
  861.6 86.4 all-reduce.22
where the time goes:
time: 1010 us; the launch traced here: 998 us
  waiting for transfers between devices  567 us (56%)
  other arithmetic  164 us (16%)
  blocking collectives  157 us (16%)
  matrix products  58.3 us (6%)
  local copies, waits for them, and re-layouts  36 us (4%)
  between operations  14.9 us (1%)
    psum x4, waiting for transfers between devices, per_device(): cols_sum = lax.psum(summed[:col_panel], 'row')  346 us
    psum x4, waiting for transfers between devices, per_device(): rows_sum = lax.psum(forward_summed[:row_panel], 'col')  221 us
    psum x4, blocking collectives, per_device(): gram = lax.psum(local_gram(projected), 'col') / total_boxes  98.2 us
    scatter-add x4, other arithmetic, per_device(): summed = jax.ops.segment_sum(product, bwd_ids, num_segments=col_panel + 1)  54.1 us
    scatter-add x4, other arithmetic, per_device(): jax.ops.segment_sum(forward_product, fwd_ids, num_segments=row_panel + 1)  54 us
    another operation x12, other arithmetic, rotate(): lower = jnp.linalg.cholesky(gram)  26.1 us
    all_gather x1, blocking collectives, per_device(): col_mass_panel = lax.all_gather(col_mass, 'row', axis=0, tiled=True)  24.9 us
    all_gather x1, blocking collectives, per_device(): lax.all_gather(vectors, 'row', axis=0, tiled=True)  23.5 us
  transfers between devices with their start and end apart: 8, of which 8 were waited for; matrix products, arithmetic and copies ran while one was open for 0% of the time, Pallas kernels for 0%

commit v1 on v0

--- a/solution.py
+++ b/solution.py
@@ -47,7 +47,12 @@
     fwd_ids = jnp.where(live, rows_idx, row_panel)
     bwd_ids = jnp.where(live, cols_idx, col_panel)
     square = tile.reshape(n_cap, bsize, bsize)
-    col_mass_panel = lax.all_gather(col_mass, "row", axis=0, tiled=True)
+    ring = [col_mass]
+    for hop in range(15):
+        ring.append(lax.ppermute(ring[-1], "row", [(dev, (dev + 1) % 16) for dev in range(16)]))
+    col_mass_panel = jnp.roll(
+        jnp.concatenate(ring[::-1], axis=0), (lax.axis_index("row") + 1) * ring[0].shape[0], axis=0
+    )
     row_mass_panel = lax.all_gather(row_mass, "col", axis=0, tiled=True)
     inv_col = 1.0 / jnp.sqrt(col_mass_panel)
     current = lax.all_gather(vectors, "row", axis=0, tiled=True).reshape(col_panel, vecs, bsize)

time: 1010 us -> 1080 us (1.069)
  waiting for transfers between devices: 567 us -> 654 us
  blocking collectives: 157 us -> 133 us
    ppermute x0 -> x15, waiting for transfers between devices: none -> 86.1 us  [per_device(): lax.ppermute(ring[-1], 'row', [(dev, (dev + 1) % 16) for dev in range(16)])]
    all_gather x1 -> x0, blocking collectives: 24.9 us -> none  [per_device(): col_mass_panel = lax.all_gather(col_mass, 'row', axis=0, tiled=True)]
  transfers between devices with their start and end apart: 8 -> 23, of which waited for: 8 -> 22; matrix products, arithmetic and copies ran while one was open for 0% -> 1% of each run, Pallas kernels for 0% -> 0%
where the time goes in v1:
time: 1080 us; the launch traced here: 1060 us
  waiting for transfers between devices  654 us (61%)
  other arithmetic  165 us (15%)
  blocking collectives  133 us (12%)
  matrix products  58.3 us (5%)
  local copies, waits for them, and re-layouts  36.2 us (3%)
  between operations  14.9 us (1%)
    psum x4, waiting for transfers between devices, per_device(): cols_sum = lax.psum(summed[:col_panel], 'row')  346 us
    psum x4, waiting for transfers between devices, per_device(): rows_sum = lax.psum(forward_summed[:row_panel], 'col')  221 us
    psum x4, blocking collectives, per_device(): gram = lax.psum(local_gram(projected), 'col') / total_boxes  97.4 us
    ppermute x15, waiting for transfers between devices, per_device(): lax.ppermute(ring[-1], 'row', [(dev, (dev + 1) % 16) for dev in range(16)])  86.1 us
    scatter-add x4, other arithmetic, per_device(): summed = jax.ops.segment_sum(product, bwd_ids, num_segments=col_panel + 1)  54.1 us
    scatter-add x4, other arithmetic, per_device(): jax.ops.segment_sum(forward_product, fwd_ids, num_segments=row_panel + 1)  54 us
    another operation x12, other arithmetic, rotate(): lower = jnp.linalg.cholesky(gram)  26.1 us
    all_gather x1, blocking collectives, per_device(): lax.all_gather(vectors, 'row', axis=0, tiled=True)  24.4 us
  transfers between devices with their start and end apart: 23, of which 22 were waited for; matrix products, arithmetic and copies ran while one was open for 1% of the time, Pallas kernels for 0%

profile of v1, /device:TPU:0, one launch (start us, length us, event | category | flops | bytes accessed | tf_op | source)
XLA Modules:
  0.0 1064.5 jit_solution(1984990714526070705)
XLA Ops:
  8.5 6.3 collective-permute-done
  14.9 6.9 collective-permute-done.1
  21.8 6.9 collective-permute-done.2
  28.6 6.9 collective-permute-done.3
  35.5 6.9 collective-permute-done.4
  43.1 6.2 collective-permute-done.5
  50.0 6.2 collective-permute-done.6
  56.9 6.2 collective-permute-done.7
  63.8 6.2 collective-permute-done.8
  70.6 6.2 collective-permute-done.9
  76.9 24.4 %all-gather = f32[16,2,4096]{2,1,0:T(2,128)S(1)} all-gather(f32[1,2,4096]{2,1,0:T(2,128)} %bitcast.99), channel_id=1, replica_groups=mesh['row'=16,'col'=8] {'row'}, dimensions={0}, use_global_device_ids=true | all-gather | bytes 557056 | tf_op jit(solution)/shard_map/all_gather | solution.py:58
  102.5 5.7 collective-permute-done.11
  108.3 6.9 collective-permute-done.12
  115.1 6.9 collective-permute-done.13
  124.3 3.0 copy.41
  132.6 4.8 fusion.14
  137.5 13.5 %scatter_fusion = f32[17,64,64]{2,1,0:T(8,128)S(1)} fusion(f32[17,64,64]{2,1,0:T(8,128)S(1)} %broadcast.83.clone.2, s32[128]{0:T(128)S(1)} %get-tuple-element.8, f32[128,64,64]{2,1,0:T(8,128)} %fusion.14), kind=kCustom, calls=%fused_computation.8 | custom fusion | flops 524288 | bytes 6291968 | tf_op jit(solution)/shard_map/scatter-add | solution.py:65
  151.9 10.8 %all-gather.1 = f32[8,2,64]{2,1,0:T(2,128)S(1)} all-gather(f32[1,2,64]{2,1,0:T(2,128)S(1)} %bitcast.100), channel_id=1, replica_groups=mesh['row'=16,'col'=8] {'col'}, dimensions={0}, use_global_device_ids=true | all-gather | bytes 4608 | tf_op jit(solution)/shard_map/all_gather | solution.py:56
  162.8 49.4 %all-reduce.9.cloned.1.call-done = f32[16,64,64]{2,1,0:T(8,128)} async-done(((f32[16,64,64]{2,1,0:T(8,128)}), f32[16,64,64]{2,1,0:T(8,128)}) %all-reduce.9.cloned.1.call-update) | async-done | bytes 262160 | tf_op jit(solution)/shard_map/psum | solution.py:66
  213.3 2.1 gather_fusion.1
  215.4 4.3 fusion.12
  219.8 13.5 %scatter_fusion.1 = f32[33,64,64]{2,1,0:T(8,128)S(1)} fusion(f32[33,64,64]{2,1,0:T(8,128)S(1)} %broadcast.82.clone.2, s32[128]{0:T(128)S(1)} %get-tuple-element.6, f32[128,64,64]{2,1,0:T(8,128)} %fusion.12), kind=kCustom, calls=%fused_computation.9 | custom fusion | flops 524288 | bytes 6291968 | tf_op jit(solution)/shard_map/scatter-add | solution.py:70
  234.5 86.6 %all-reduce.11.cloned.1.call-done = f32[32,64,64]{2,1,0:T(8,128)} async-done(((f32[32,64,64]{2,1,0:T(8,128)}), f32[32,64,64]{2,1,0:T(8,128)}) %all-reduce.11.cloned.1.call-update) | async-done | bytes 524304 | tf_op jit(solution)/shard_map/psum | solution.py:71
  321.1 2.7 convolution_bitcast_fusion.7
  323.9 24.1 %psum.86 = f32[64,64]{0,1:T(8,128)S(1)} all-reduce(f32[64,64]{0,1:T(8,128)S(1)} %convolution_bitcast_fusion.7), channel_id=1, replica_groups=mesh['row'=16,'col'=8] {'col'}, use_global_device_ids=true, to_apply=%region_4.7 | all-reduce | flops 4096 | bytes 32768 | tf_op jit(solution)/shard_map/psum | solution.py:73
  348.1 5.8 cholesky.74
  355.3 4.9 custom-call.8
  360.4 2.8 fusion.29
  364.5 2.1 gather_fusion.2
  366.7 4.8 fusion.10
  371.5 13.5 %scatter_fusion.2 = f32[17,64,64]{2,1,0:T(8,128)S(1)} fusion(f32[17,64,64]{2,1,0:T(8,128)S(1)} %broadcast.83.clone.1, s32[128]{0:T(128)S(1)} %get-tuple-element.8, f32[128,64,64]{2,1,0:T(8,128)} %fusion.10), kind=kCustom, calls=%fused_computation.10 | custom fusion | flops 524288 | bytes 6291968 | tf_op jit(solution)/shard_map/scatter-add | solution.py:65
  386.0 57.4 %all-reduce.13.cloned.1.call-done = f32[16,64,64]{2,1,0:T(8,128)} async-done(((f32[16,64,64]{2,1,0:T(8,128)}), f32[16,64,64]{2,1,0:T(8,128)}) %all-reduce.13.cloned.1.call-update) | async-done | bytes 262160 | tf_op jit(solution)/shard_map/psum | solution.py:66
  446.6 4.3 fusion.8
  451.0 13.5 %scatter_fusion.3 = f32[33,64,64]{2,1,0:T(8,128)S(1)} fusion(f32[33,64,64]{2,1,0:T(8,128)S(1)} %broadcast.82.clone.1, s32[128]{0:T(128)S(1)} %get-tuple-element.6, f32[128,64,64]{2,1,0:T(8,128)} %fusion.8), kind=kCustom, calls=%fused_computation.11 | custom fusion | flops 524288 | bytes 6291968 | tf_op jit(solution)/shard_map/scatter-add | solution.py:70
  465.9 86.4 %all-reduce.15.cloned.1.call-done = f32[32,64,64]{2,1,0:T(8,128)} async-done(((f32[32,64,64]{2,1,0:T(8,128)}), f32[32,64,64]{2,1,0:T(8,128)}) %all-reduce.15.cloned.1.call-update) | async-done | bytes 524304 | tf_op jit(solution)/shard_map/psum | solution.py:71
  552.3 2.7 convolution_bitcast_fusion.5
  555.0 24.1 %psum.89 = f32[64,64]{0,1:T(8,128)S(1)} all-reduce(f32[64,64]{0,1:T(8,128)S(1)} %convolution_bitcast_fusion.5), channel_id=1, replica_groups=mesh['row'=16,'col'=8] {'col'}, use_global_device_ids=true, to_apply=%region_11.16 | all-reduce | flops 4096 | bytes 32768 | tf_op jit(solution)/shard_map/psum | solution.py:73
  579.3 5.8 cholesky.85
  586.5 4.9 custom-call.9
  591.6 2.8 fusion.28
  595.7 2.1 gather_fusion.4
  597.9 4.8 fusion.6
  602.7 13.5 %scatter_fusion.4 = f32[17,64,64]{2,1,0:T(8,128)S(1)} fusion(f32[17,64,64]{2,1,0:T(8,128)S(1)} %broadcast.83.clone, s32[128]{0:T(128)S(1)} %get-tuple-element.8, f32[128,64,64]{2,1,0:T(8,128)} %fusion.6), kind=kCustom, calls=%fused_computation.12 | custom fusion | flops 524288 | bytes 6291968 | tf_op jit(solution)/shard_map/scatter-add | solution.py:65
  617.1 57.4 %all-reduce.17.cloned.1.call-done = f32[16,64,64]{2,1,0:T(8,128)} async-done(((f32[16,64,64]{2,1,0:T(8,128)}), f32[16,64,64]{2,1,0:T(8,128)}) %all-reduce.17.cloned.1.call-update) | async-done | bytes 262160 | tf_op jit(solution)/shard_map/psum | solution.py:66
  675.6 2.1 gather_fusion.5
  677.7 4.3 fusion.4
  682.1 13.5 %scatter_fusion.5 = f32[33,64,64]{2,1,0:T(8,128)S(1)} fusion(f32[33,64,64]{2,1,0:T(8,128)S(1)} %broadcast.82.clone, s32[128]{0:T(128)S(1)} %get-tuple-element.6, f32[128,64,64]{2,1,0:T(8,128)} %fusion.4), kind=kCustom, calls=%fused_computation.13 | custom fusion | flops 524288 | bytes 6291968 | tf_op jit(solution)/shard_map/scatter-add | solution.py:70
  696.8 86.6 %all-reduce.19.cloned.1.call-done = f32[32,64,64]{2,1,0:T(8,128)} async-done(((f32[32,64,64]{2,1,0:T(8,128)}), f32[32,64,64]{2,1,0:T(8,128)}) %all-reduce.19.cloned.1.call-update) | async-done | bytes 524304 | tf_op jit(solution)/shard_map/psum | solution.py:71
  783.5 2.7 convolution_bitcast_fusion.3
  786.2 24.7 %psum.92 = f32[64,64]{0,1:T(8,128)S(1)} all-reduce(f32[64,64]{0,1:T(8,128)S(1)} %convolution_bitcast_fusion.3), channel_id=1, replica_groups=mesh['row'=16,'col'=8] {'col'}, use_global_device_ids=true, to_apply=%region_16.21 | all-reduce | flops 4096 | bytes 32768 | tf_op jit(solution)/shard_map/psum | solution.py:73
  811.0 5.8 cholesky.96
  818.2 4.9 custom-call.10
  823.3 2.8 fusion.27
  827.4 2.1 gather_fusion.6
  829.6 4.8 fusion.2
  834.4 13.5 %scatter_fusion.6 = f32[17,64,64]{2,1,0:T(8,128)S(1)} fusion(f32[17,64,64]{2,1,0:T(8,128)S(1)} %broadcast.83, s32[128]{0:T(128)S(1)} %get-tuple-element.8, f32[128,64,64]{2,1,0:T(8,128)} %fusion.2), kind=kCustom, calls=%fused_computation.14 | custom fusion | flops 524288 | bytes 6291968 | tf_op jit(solution)/shard_map/scatter-add | solution.py:65
  848.8 57.4 %all-reduce.21.cloned.1.call-done = f32[16,64,64]{2,1,0:T(8,128)} async-done(((f32[16,64,64]{2,1,0:T(8,128)}), f32[16,64,64]{2,1,0:T(8,128)}) %all-reduce.21.cloned.1.call-update) | async-done | bytes 262160 | tf_op jit(solution)/shard_map/psum | solution.py:66
  909.5 4.3 fusion
  913.8 13.5 %scatter_fusion.7 = f32[33,64,64]{2,1,0:T(8,128)S(1)} fusion(f32[33,64,64]{2,1,0:T(8,128)S(1)} %broadcast.82, s32[128]{0:T(128)S(1)} %get-tuple-element.6, f32[128,64,64]{2,1,0:T(8,128)} %fusion), kind=kCustom, calls=%fused_computation.15 | custom fusion | flops 524288 | bytes 6291968 | tf_op jit(solution)/shard_map/scatter-add | solution.py:70
  928.6 86.6 %all-reduce.23.cloned.1.call-done = f32[32,64,64]{2,1,0:T(8,128)} async-done(((f32[32,64,64]{2,1,0:T(8,128)}), f32[32,64,64]{2,1,0:T(8,128)}) %all-reduce.23.cloned.1.call-update) | async-done | bytes 524304 | tf_op jit(solution)/shard_map/psum | solution.py:71
  1015.2 2.7 convolution_bitcast_fusion.1
  1017.9 24.4 %psum.95 = f32[64,64]{0,1:T(8,128)S(1)} all-reduce(f32[64,64]{0,1:T(8,128)S(1)} %convolution_bitcast_fusion.1), channel_id=1, replica_groups=mesh['row'=16,'col'=8] {'col'}, use_global_device_ids=true, to_apply=%region_21.26 | all-reduce | flops 4096 | bytes 32768 | tf_op jit(solution)/shard_map/psum | solution.py:73
  1042.5 5.8 cholesky.107
  1049.7 4.9 custom-call.11
  (119 shorter events, 44.5 us)
Async XLA Ops:
  6.5 117.1 %copy-start.4 = (bf16[1,1,128,4096]{3,2,1,0:T(8,128)(2,1)S(1)}, bf16[1,1,128,4096]{3,2,1,0:T(8,128)(2,1)}, u32[]{:S(2)}) copy-start(bf16[1,1,128,4096]{3,2,1,0:T(8,128)(2,1)} %param.14) | copy-start | bytes 3145732
  6.5 205.6 %all-reduce.9.cloned.1.call-start = ((), (), s32[]{:S(2)}) async-start(), calls=%async_computation | async-start | bytes 1048576 | tf_op jit(solution)/shard_map/psum | solution.py:66
  6.5 8.3 collective-permute-start
  14.9 6.9 collective-permute-start.1
  21.8 6.9 collective-permute-start.2
  28.6 6.9 collective-permute-start.3
  35.5 6.9 collective-permute-start.4
  42.4 6.9 collective-permute-start.5
  49.3 6.9 collective-permute-start.6
  56.2 6.9 collective-permute-start.7
  63.1 6.9 collective-permute-start.8
  70.0 6.9 collective-permute-start.9
  76.9 24.4 %collective-permute-start.10 = (f32[2,64]{1,0:T(2,128)S(1)}, f32[2,64]{1,0:T(2,128)S(1)}, u32[]{:S(2)}, u32[]{:S(2)}) collective-permute-start(f32[2,64]{1,0:T(2,128)S(1)} %collective-permute-done.9), channel_id=1, source_target_pairs={{0,8},{8,16},{16,24},{24,32},{32,40},{40,48},{48,56},{56,64},{64,7... | collective-permute-start | bytes 1544 | tf_op jit(solution)/shard_map/ppermute | solution.py:52
  101.3 7.0 collective-permute-start.11
  108.2 6.9 collective-permute-start.12
  115.1 6.9 collective-permute-start.13
  122.0 6.9 collective-permute-start.14
  124.3 4.6 copy-start.5
  137.4 14.5 %copy-start.7 = (s32[1,1,128]{2,1,0:T(1,128)S(1)}, s32[1,1,128]{2,1,0:T(1,128)}, u32[]{:S(2)}) copy-start(s32[1,1,128]{2,1,0:T(1,128)} %param.15) | copy-start | bytes 1540
  137.5 14.5 %copy-start.6 = (f32[2,64]{1,0:T(2,128)S(1)}, f32[2,64]{1,0:T(2,128)}, u32[]{:S(2)}) copy-start(f32[2,64]{1,0:T(2,128)} %param.19) | copy-start | bytes 1540
  151.9 169.2 %all-reduce.11.cloned.1.call-start = ((), (), s32[]{:S(2)}) async-start(), calls=%async_computation.1 | async-start | bytes 2097152 | tf_op jit(solution)/shard_map/psum | solution.py:71
  234.5 208.9 %all-reduce.13.cloned.1.call-start = ((), (), s32[]{:S(2)}) async-start(), calls=%async_computation.2 | async-start | bytes 1048576 | tf_op jit(solution)/shard_map/psum | solution.py:66
  321.1 39.3 %copy-start.1 = (f32[32,64,64]{2,1,0:T(8,128)S(1)}, f32[32,64,64]{2,1,0:T(8,128)}, u32[]{:S(2)}) copy-start(f32[32,64,64]{2,1,0:T(8,128)} %all-reduce.11.cloned.1.call-done) | copy-start | bytes 1572868
  385.9 166.4 %all-reduce.15.cloned.1.call-start = ((), (), s32[]{:S(2)}) async-start(), calls=%async_computation.3 | async-start | bytes 2097152 | tf_op jit(solution)/shard_map/psum | solution.py:71
  465.6 208.9 %all-reduce.17.cloned.1.call-start = ((), (), s32[]{:S(2)}) async-start(), calls=%async_computation.4 | async-start | bytes 1048576 | tf_op jit(solution)/shard_map/psum | solution.py:66
  552.3 39.3 %copy-start.2 = (f32[32,64,64]{2,1,0:T(8,128)S(1)}, f32[32,64,64]{2,1,0:T(8,128)}, u32[]{:S(2)}) copy-start(f32[32,64,64]{2,1,0:T(8,128)} %all-reduce.15.cloned.1.call-done) | copy-start | bytes 1572868
  617.1 166.4 %all-reduce.19.cloned.1.call-start = ((), (), s32[]{:S(2)}) async-start(), calls=%async_computation.5 | async-start | bytes 2097152 | tf_op jit(solution)/shard_map/psum | solution.py:71
  696.8 209.4 %all-reduce.21.cloned.1.call-start = ((), (), s32[]{:S(2)}) async-start(), calls=%async_computation.6 | async-start | bytes 1048576 | tf_op jit(solution)/shard_map/psum | solution.py:66
  783.5 39.9 %copy-start.3 = (f32[32,64,64]{2,1,0:T(8,128)S(1)}, f32[32,64,64]{2,1,0:T(8,128)}, u32[]{:S(2)}) copy-start(f32[32,64,64]{2,1,0:T(8,128)} %all-reduce.19.cloned.1.call-done) | copy-start | bytes 1572868
  848.8 166.4 %all-reduce.23.cloned.1.call-start = ((), (), s32[]{:S(2)}) async-start(), calls=%async_computation.7 | async-start | bytes 2097152 | tf_op jit(solution)/shard_map/psum | solution.py:71
  1015.2 39.6 %copy-start = (f32[32,64,64]{2,1,0:T(8,128)S(1)}, f32[32,64,64]{2,1,0:T(8,128)}, u32[]{:S(2)}) copy-start(f32[32,64,64]{2,1,0:T(8,128)} %all-reduce.23.cloned.1.call-done) | copy-start | bytes 1572868
Sparse Core Ops, SparseCore 0:
  152.0 60.1 all-reduce.8
  234.6 86.4 all-reduce.10
  386.0 57.2 all-reduce.12
  465.8 86.4 all-reduce.14
  617.2 57.2 all-reduce.16
  696.9 86.5 all-reduce.18
  848.9 57.2 all-reduce.20
  928.7 86.4 all-reduce.22
